TPU v7x, 128 devices: a whole 4x4x4 slice. The times are simulated.
128 devices in a mesh: dp: 16 (over x_lo, z, core), mp: 8 (over x_hi, y).
Axes of the slice: x: 4 (x_hi: 2, x_lo: 2; x = x_hi * 2 + x_lo), y: 4, z: 4, core: 2. Of those that a mesh axis runs over, the one named last changes fastest.
Arguments:
- tokens: bfloat16 [8192, 1280], P('dp'), may hold values from -6 to 6
- norm_gain: float32 [1280], replicated, may hold values from 0.25 to 1.75
- widen_weight: bfloat16 [1280, 5120], P(None, 'mp'), may hold values from -0.15625 to 0.15625
- narrow_weight: bfloat16 [5120, 1280], P('mp'), may hold values from -0.078125 to 0.078125
- final_gain: float32 [1280], replicated, may hold values from 0.25 to 1.75
- adaptor_in: bfloat16 [3, 1280, 1280], P(None, None, 'mp'), may hold values from -0.15625 to 0.15625
- head_dino: bfloat16 [1280, 1536], P('mp'), may hold values from -0.15625 to 0.15625
- head_siglip: bfloat16 [1280, 1152], P('mp'), may hold values from -0.15625 to 0.15625
- head_sam: bfloat16 [1280, 1280], P('mp'), may hold values from -0.15625 to 0.15625
- teacher_dino: bfloat16 [2, 8192, 1536], P(None, 'dp', 'mp'), may hold values from -6 to 6
- teacher_siglip: bfloat16 [2, 8192, 1152], P(None, 'dp', 'mp'), may hold values from -6 to 6
- teacher_sam: bfloat16 [2, 8192, 1280], P(None, 'dp', 'mp'), may hold values from -6 to 6
- step_lags: int32 [3], replicated, may hold values from 1 to 2, as said below
- owner_slot: int32 [256], replicated, may hold values from 0 to 255, as said below
Outputs:
- grad_widen: float32 [5120, 1280], P('mp', 'dp')
- grad_narrow: float32 [5120, 1280], P('mp', 'dp')
- grad_adaptor: float32 [3, 1280, 1280], P(None, 'dp', 'mp')
- grad_dino: float32 [1280, 1536], P('mp', 'dp')
- grad_siglip: float32 [1280, 1152], P('mp', 'dp')
- grad_sam: float32 [1280, 1280], P('mp', 'dp')
Inputs may be any that keep to these rules, and one draw needn't show every extreme that they name: owner_slot is a permutation; of the 16 images in each aligned block of 16 images, exactly 1 have slots in each aligned block of 16 slots. `step_lags`: the three lags are not all equal.
All inputs are finite; a program needn't handle non-finite values.
Results may differ from a plain program's by a relative error of at most 0.02.
Values may be sent and summed in bfloat16 or wider, within the bound.
A program may use at most 128 MiB of HBM per device.

v0:
```python
import jax
import jax.numpy as jnp
from jax import lax
from jax.sharding import PartitionSpec as P

PATCH = 32


slope_coef = 0.7978845608028654
cubic_coef = 0.044715


def in_one_piece(arrays, axis, split_dim, concat_dim, along):
    widths = [a.shape[along] for a in arrays]
    both = jnp.concatenate(arrays, axis=along)
    filled = lax.all_to_all(both, axis, split_axis=split_dim, concat_axis=concat_dim, tiled=True)
    return tuple(jnp.split(filled, [sum(widths[:k]) for k in range(1, len(widths))], axis=along))


def from_everyone(shard, axis):
    size = lax.axis_size(axis)
    return lax.all_to_all(
        jnp.broadcast_to(shard[None], (size, *shard.shape)), axis, 0, 0, tiled=True
    )


def taken_together(shard, axis):
    everything = from_everyone(shard, axis)
    return jnp.sum(everything, axis=0)


def joined_along(pieces, dim):
    shape = list(pieces.shape[1:])
    shape[dim] *= pieces.shape[0]
    return jnp.moveaxis(pieces, 0, dim).reshape(shape)


def gather_packed(arrays, axis, dims):
    vector = jnp.concatenate([a.reshape(-1) for a in arrays])
    lines, at, done = (lax.all_gather(vector, axis), 0, [])
    for a, dim in zip(arrays, dims):
        pieces = lines[:, at : at + a.size].reshape(-1, *a.shape)
        done.append(joined_along(pieces, dim))
        at += a.size
    return tuple(done)


def for_sending(shard):
    return jax.tree.map(lambda a: a.astype(jnp.bfloat16) if a.dtype == jnp.float32 else a, shard)


def in_blocks(shard, dim, size):
    shape = shard.shape
    pieces = shard.reshape(*shape[:dim], size, shape[dim] // size, *shape[dim + 1 :])
    return jnp.moveaxis(pieces, dim, 0)


def sent_and_summed(shard, axis, dim):
    pieces = in_blocks(shard, dim, lax.axis_size(axis))
    arrived = lax.all_to_all(pieces, axis, split_axis=0, concat_axis=0, tiled=True)
    return arrived.astype(jnp.float32).sum(axis=0)


def collect(shard, axis, dim):
    return joined_along(from_everyone(shard, axis), dim)


def side_by_side(arrays, axis, dim, along):
    widths = [a.shape[along] for a in arrays]
    both = jnp.concatenate(arrays, axis=along)
    filled = lax.psum_scatter(both, axis, scatter_dimension=dim, tiled=True)
    return tuple(jnp.split(filled, [sum(widths[:k]) for k in range(1, len(widths))], axis=along))


def smooth(value):
    return 0.5 * value * (1.0 + jnp.tanh(slope_coef * (value + cubic_coef * value * value * value)))


def smooth_slope(value):
    tangent = jnp.tanh(slope_coef * (value + cubic_coef * value * value * value))
    return 0.5 * (1.0 + tangent) + 0.5 * value * (1.0 - tangent * tangent) * slope_coef * (
        1.0 + 3.0 * cubic_coef * value * value
    )


def normalize(value, gain):
    centre = value - jnp.mean(value, axis=-1, keepdims=True)
    inverse = lax.rsqrt(jnp.mean(centre * centre, axis=-1, keepdims=True) + 1e-06)
    normal = centre * inverse
    return (normal * gain, normal, inverse)


def normalize_back(upstream, gain, normal, inverse):
    scaled = upstream * gain
    return inverse * (
        scaled
        - jnp.mean(scaled, axis=-1, keepdims=True)
        - normal * jnp.mean(scaled * normal, axis=-1, keepdims=True)
    )


def finish(product, square_student, square_target, student, target):
    joint = lax.rsqrt(square_student * square_target)
    cosine = product * joint
    slope = cosine[:, None] * student / square_student[:, None] - target * joint[:, None]
    return (cosine, slope)


def column_terms(students, targets):
    return jnp.stack(
        [
            jnp.stack(
                [
                    jnp.sum(students[index] * targets[index], axis=-1),
                    jnp.sum(students[index] * students[index], axis=-1),
                    jnp.sum(targets[index] * targets[index], axis=-1),
                ]
            )
            for index in range(3)
        ]
    )


def column_finish(summed_terms, students, targets):
    local_slopes = []
    for index in range(3):
        cosine, slope = finish(
            summed_terms[index, 0],
            summed_terms[index, 1] + 1e-06,
            summed_terms[index, 2] + 1e-06,
            students[index],
            targets[index],
        )
        local_slopes.append(slope.astype(jnp.bfloat16))
    return local_slopes


def local(
    tokens,
    norm_gain,
    widen_weight,
    narrow_weight,
    final_gain,
    adaptor_in,
    head_dino,
    head_siglip,
    head_sam,
    teacher_dino,
    teacher_siglip,
    teacher_sam,
    step_lags,
    owner_slot,
):
    groups = lax.axis_size("dp")
    members = lax.axis_size("mp")
    group = lax.axis_index("dp")
    member = lax.axis_index("mp")
    rows = tokens.shape[0]
    images = rows // PATCH
    share = images // groups
    block = rows // members
    heads = (head_dino, head_siglip, head_sam)
    mine = lax.dynamic_slice_in_dim(owner_slot, group * images, images)
    sending = jnp.argsort(mine)
    outgoing = []
    for index, teacher in enumerate((teacher_dino, teacher_siglip, teacher_sam)):
        stale = lax.dynamic_index_in_dim(teacher, step_lags[index] - 1, 0, keepdims=False)
        width = stale.shape[-1]
        ordered = jnp.take(stale.reshape(images, PATCH, width), sending, axis=0)
        outgoing.append(ordered)
    arrived = in_one_piece((outgoing[0], outgoing[1], outgoing[2]), "dp", 0, 0, 2)
    ranked = jnp.sort(owner_slot.reshape(groups, images), axis=1)
    landed = (
        lax.dynamic_slice_in_dim(ranked, group * share, share, 1).reshape(images) - group * images
    )
    placing = jnp.argsort(landed)
    owned = [jnp.take(piece, placing, axis=0) for piece in arrived]
    first, normal_one, inverse_one = normalize(tokens.astype(jnp.float32), norm_gain)
    first = first.astype(jnp.bfloat16)
    widened = jnp.dot(first, widen_weight, preferred_element_type=jnp.float32)
    active = smooth(widened).astype(jnp.bfloat16)
    mixed = jnp.dot(active, narrow_weight, preferred_element_type=jnp.float32)
    hidden = tokens.astype(jnp.float32) + lax.psum(mixed, "mp")
    final, normal_two, inverse_two = normalize(hidden, final_gain)
    final = final.astype(jnp.bfloat16)
    before = jnp.einsum("rd,tdh->trh", final, adaptor_in, preferred_element_type=jnp.float32)
    lifted = smooth(before).astype(jnp.bfloat16)
    targets = [piece.reshape(rows, piece.shape[-1]).astype(jnp.float32) for piece in owned]
    whole_lifted = lax.all_gather(lifted, "mp", axis=2, tiled=True)
    head_columns = (
        lax.all_to_all(head_dino, "mp", split_axis=1, concat_axis=0, tiled=True),
        lax.all_to_all(head_siglip, "mp", split_axis=1, concat_axis=0, tiled=True),
        lax.all_to_all(head_sam, "mp", split_axis=1, concat_axis=0, tiled=True),
    )
    students = [
        jnp.dot(whole_lifted[index], head_columns[index], preferred_element_type=jnp.float32)
        for index in range(3)
    ]
    summed_terms = taken_together(column_terms(students, targets), "mp")
    local_slopes = column_finish(summed_terms, students, targets)
    slopes = gather_packed((local_slopes[0], local_slopes[1], local_slopes[2]), "mp", (1, 1, 1))
    column_grads = tuple(
        (
            jnp.einsum(
                "rh,rc->hc",
                whole_lifted[index],
                local_slopes[index],
                preferred_element_type=jnp.float32,
            )
            for index in range(3)
        )
    )
    head_grads = list(
        jax.tree.map(
            lambda part, own: part.astype(own.dtype),
            lax.all_to_all(
                for_sending(column_grads), "mp", split_axis=0, concat_axis=1, tiled=True
            ),
            column_grads,
        )
    )
    back = jnp.stack(
        [
            jnp.einsum("rc,hc->rh", slopes[index], heads[index], preferred_element_type=jnp.float32)
            for index in range(3)
        ]
    )
    inner = (back * smooth_slope(before)).astype(jnp.bfloat16)
    grad_adaptor = jnp.einsum("rd,trh->tdh", final, inner, preferred_element_type=jnp.float32)
    upstream_part = jnp.einsum("trh,tdh->rd", inner, adaptor_in, preferred_element_type=jnp.float32)
    upstream = sent_and_summed(upstream_part.astype(jnp.bfloat16), "mp", 0)
    normal_rows = lax.dynamic_slice_in_dim(normal_two, member * block, block, 0)
    inverse_rows = lax.dynamic_slice_in_dim(inverse_two, member * block, block, 0)
    through_rows = normalize_back(upstream, final_gain, normal_rows, inverse_rows).astype(
        jnp.bfloat16
    )
    through = collect(through_rows, "mp", 0)
    grad_narrow = jnp.einsum("rf,rd->fd", active, through, preferred_element_type=jnp.float32)
    back_two = jnp.einsum("rd,fd->rf", through, narrow_weight, preferred_element_type=jnp.float32)
    inner_two = (back_two * smooth_slope(widened)).astype(jnp.bfloat16)
    grad_widen = jnp.einsum("rf,rd->fd", inner_two, first, preferred_element_type=jnp.float32)
    reduced = (
        *tuple(
            (
                part.astype(jnp.float32)
                for part in side_by_side(
                    (grad_widen.astype(jnp.bfloat16), grad_narrow.astype(jnp.bfloat16)), "dp", 1, 0
                )
            )
        ),
        lax.psum_scatter(
            grad_adaptor.astype(jnp.bfloat16), "dp", scatter_dimension=1, tiled=True
        ).astype(jnp.float32),
        lax.psum_scatter(
            head_grads[0].astype(jnp.bfloat16), "dp", scatter_dimension=1, tiled=True
        ).astype(jnp.float32),
        lax.psum_scatter(
            head_grads[1].astype(jnp.bfloat16), "dp", scatter_dimension=1, tiled=True
        ).astype(jnp.float32),
        lax.psum_scatter(
            head_grads[2].astype(jnp.bfloat16), "dp", scatter_dimension=1, tiled=True
        ).astype(jnp.float32),
    )
    return (reduced[0], reduced[1], reduced[2], reduced[3], reduced[4], reduced[5])


def solution(mesh):
    placed = (
        P("dp", None),
        P(),
        P(None, "mp"),
        P("mp", None),
        P(),
        P(None, None, "mp"),
        P("mp", None),
        P("mp", None),
        P("mp", None),
        P(None, "dp", "mp"),
        P(None, "dp", "mp"),
        P(None, "dp", "mp"),
        P(),
        P(),
    )
    return jax.shard_map(
        local,
        mesh=mesh,
        in_specs=placed,
        out_specs=(
            P("mp", "dp"),
            P("mp", "dp"),
            P(None, "dp", "mp"),
            P("mp", "dp"),
            P("mp", "dp"),
            P("mp", "dp"),
        ),
        check_vma=False,
    )
```

profile of v0, /device:TPU:24, one launch (start us, length us, event | category | flops | bytes accessed | tf_op | source)
XLA Modules:
  0.0 680.0 jit_solution(16795986844906720179)
XLA Ops:
  16.3 96.1 %all-reduce.2.cloned.1.call-done = f32[512,1280]{1,0:T(8,128)} async-done(((f32[512,1280]{1,0:T(8,128)}), f32[512,1280]{1,0:T(8,128)}) %all-reduce.2.cloned.1.call-update) | async-done | bytes 2621456 | tf_op jit(solution)/shard_map/psum | solution.py:183
  120.8 6.2 all-to-all-start.2
  170.1 7.2 %all-to-all-start.3 = ((bf16[160,8,160]{0,2,1:T(8,128)(2,1)}), bf16[160,8,160]{0,2,1:T(8,128)(2,1)}, u32[]{:S(2)}, u32[]{:S(2)}) async-start(bf16[160,8,160]{0,2,1:T(8,128)(2,1)} %bitcast.150), calls=%async_computation.3 | async-start | bytes 1310720 | tf_op jit(solution)/shard_map/all_to_all | solution.py:193
  180.5 6.1 all-to-all-done.3
  202.0 7.3 %all-to-all-start = ((bf16[160,8,192]{2,0,1:T(8,128)(2,1)}), bf16[160,8,192]{2,0,1:T(8,128)(2,1)}, u32[]{:S(2)}, u32[]{:S(2)}) async-start(bf16[160,8,192]{2,0,1:T(8,128)(2,1)} %copy.134), calls=%async_computation | async-start | bytes 1310720 | tf_op jit(solution)/shard_map/all_to_all | solution.py:191
  236.3 13.1 %all_to_all.134 = f32[8,3,3,512]{3,2,1,0:T(4,128)S(1)} all-to-all(f32[8,3,3,512]{3,2,1,0:T(4,128)S(1)} %broadcast_in_dim.31), channel_id=1, replica_groups=mesh['dp'=16,'mp'=8] {'mp'}, dimensions={0} | all-to-all | bytes 294912 | tf_op jit(solution)/shard_map/all_to_all | solution.py:22
  268.5 5.8 all-to-all-start.8
  287.2 6.5 all-to-all-start.9
  294.3 39.3 %all-gather.6.cloned.1.call-done = bf16[2031616]{0:T(1024)(128)(2,1)} async-done(((bf16[253952]{0:T(1024)(128)(2,1)}), bf16[2031616]{0:T(1024)(128)(2,1)}) %all-gather.6.cloned.1.call-update) | async-done | bytes 4063248 | tf_op jit(solution)/shard_map/all_gather | solution.py:40
  333.6 5.8 reshape.330
  349.7 5.2 reshape.273
  372.9 4.6 reshape.275
  386.6 6.5 all-to-all-start.7
  397.2 6.0 all-to-all-done.7
  403.2 6.1 all-to-all-start.5
  413.0 13.2 %all-to-all-done.5 = bf16[8,64,1280]{2,1,0:T(8,128)(2,1)} async-done(((bf16[8,64,1280]{2,1,0:T(8,128)(2,1)}), bf16[8,64,1280]{2,1,0:T(8,128)(2,1)}, u32[]{:S(2)}, u32[]{:S(2)}) %all-to-all-start.5) | async-done | bytes 1310752 | tf_op jit(solution)/shard_map/all_to_all | solution.py:60
  431.2 5.2 all-to-all-start.6
  440.3 4.9 copy.167
  445.2 6.0 reshape.355
  459.2 5.8 convolution_convert_fusion.1
  468.9 5.7 copy.165
  477.8 61.3 %reduce-scatter.20.cloned.1.call-done = bf16[96,160]{1,0:T(8,128)(2,1)} async-done(((bf16[1536,160]{1,0:T(8,128)(2,1)}), bf16[96,160]{1,0:T(8,128)(2,1)}) %reduce-scatter.20.cloned.1.call-update) | async-done | bytes 30736
  540.7 62.2 %reduce-scatter.18.cloned.1.call-done = bf16[80,480]{1,0:T(8,128)(2,1)} async-done(((bf16[1280,480]{1,0:T(8,128)(2,1)}), bf16[80,480]{1,0:T(8,128)(2,1)}) %reduce-scatter.18.cloned.1.call-update) | async-done | bytes 76816
  604.9 64.9 %reduce-scatter.16.cloned.1.call-done = bf16[80,1280]{1,0:T(8,128)(2,1)} async-done(((bf16[1280,1280]{1,0:T(8,128)(2,1)}), bf16[80,1280]{1,0:T(8,128)(2,1)}) %reduce-scatter.16.cloned.1.call-update) | async-done | bytes 204816
  (234 shorter events, 210.0 us)
Async XLA Ops:
  7.2 6.1 copy-start
  7.2 105.2 %all-reduce.2.cloned.1.call-start = ((), (), s32[]{:S(2)}) async-start(), calls=%async_computation.15 | async-start | bytes 5242880 | tf_op jit(solution)/shard_map/psum | solution.py:183
  16.3 212.2 %all-gather.4.cloned.1.call-start = ((), (), s32[]{:S(2)}) async-start(), calls=%async_computation.16 | async-start | bytes 4423680 | tf_op jit(solution)/shard_map/all_gather | solution.py:189
  119.7 7.3 %copy-start.27 = (s32[3]{0:T(128)S(1)}, s32[3]{0:T(128)}, u32[]{:S(2)}) copy-start(s32[3]{0:T(128)} %param.32) | copy-start | bytes 40
  119.7 11.8 %copy-start.30 = (s32[256]{0:T(256)S(1)}, s32[256]{0:T(256)}, u32[]{:S(2)}) copy-start(s32[256]{0:T(256)} %param.33) | copy-start | bytes 3076
  120.8 49.3 %all-to-all-start.2 = ((bf16[160,8,144]{0,2,1:T(8,128)(2,1)}), bf16[160,8,144]{0,2,1:T(8,128)(2,1)S(1)}, u32[]{:S(2)}, u32[]{:S(2)}) async-start(bf16[160,8,144]{0,2,1:T(8,128)(2,1)} %bitcast.153), calls=%async_computation.2 | async-start | bytes 1179648 | tf_op jit(solution)/shard_map/all_to_all | solution.py:192
  170.1 10.4 %copy-start.8 = (bf16[160,8,144]{0,2,1:T(8,128)(2,1)}, bf16[160,8,144]{0,2,1:T(8,128)(2,1)S(1)}, u32[]{:S(2)}) copy-start(bf16[160,8,144]{0,2,1:T(8,128)(2,1)S(1)} %all-to-all-done.2) | copy-start | bytes 1105924
  170.1 16.5 %all-to-all-start.3 = ((bf16[160,8,160]{0,2,1:T(8,128)(2,1)}), bf16[160,8,160]{0,2,1:T(8,128)(2,1)}, u32[]{:S(2)}, u32[]{:S(2)}) async-start(bf16[160,8,160]{0,2,1:T(8,128)(2,1)} %bitcast.150), calls=%async_computation.3 | async-start | bytes 1310720 | tf_op jit(solution)/shard_map/all_to_all | solution.py:193
  178.3 12.8 %copy-start.33 = (s32[16]{0:T(128)S(1)}, s32[16]{0:T(128)}, u32[]{:S(2)}) copy-start(s32[16]{0:T(128)} %get-tuple-element.15) | copy-start | bytes 196
  186.6 15.4 %all-to-all-start.1 = ((bf16[16,32,496]{2,1,0:T(8,128)(2,1)}), bf16[16,32,496]{2,1,0:T(8,128)(2,1)S(1)}, u32[]{:S(2)}, u32[]{:S(2)}) async-start(bf16[16,32,496]{2,1,0:T(8,128)(2,1)} %pad_maximum_fusion.1), calls=%async_computation.1 | async-start | bytes 1048576 | tf_op jit(solution)/shard_map/all_to_all | solution.py:16
  202.0 29.1 %all-to-all-start = ((bf16[160,8,192]{2,0,1:T(8,128)(2,1)}), bf16[160,8,192]{2,0,1:T(8,128)(2,1)}, u32[]{:S(2)}, u32[]{:S(2)}) async-start(bf16[160,8,192]{2,0,1:T(8,128)(2,1)} %copy.134), calls=%async_computation | async-start | bytes 1310720 | tf_op jit(solution)/shard_map/all_to_all | solution.py:191
  209.3 124.3 %all-gather.6.cloned.1.call-start = ((), (), s32[]{:S(2)}) async-start(), calls=%async_computation.18 | async-start | bytes 4571136 | tf_op jit(solution)/shard_map/all_gather | solution.py:40
  216.4 5.7 copy-start.9
  268.5 18.7 %all-to-all-start.8 = ((bf16[8,160,144]{1,2,0:T(8,128)(2,1)}), bf16[8,160,144]{1,2,0:T(8,128)(2,1)S(1)}, u32[]{:S(2)}, u32[]{:S(2)}) async-start(bf16[8,160,144]{1,2,0:T(8,128)(2,1)} %copy.158), calls=%async_computation.8 | async-start | bytes 1179648 | tf_op jit(solution)/shard_map/all_to_all | solution.py:216
  287.2 6.7 copy-start.7
  287.2 99.4 %all-to-all-start.9 = ((bf16[8,160,160]{1,2,0:T(8,128)(2,1)}), bf16[8,160,160]{1,2,0:T(8,128)(2,1)}, u32[]{:S(2)}, u32[]{:S(2)}) async-start(bf16[8,160,160]{1,2,0:T(8,128)(2,1)} %copy.159), calls=%async_computation.10 | async-start | bytes 1310720 | tf_op jit(solution)/shard_map/all_to_all | solution.py:216
  293.7 180.9 %reduce-scatter.14.cloned.1.call-start = ((), (), s32[]{:S(2)}) async-start(), calls=%async_computation.17 | async-start | bytes 626688 | tf_op jit(solution)/shard_map/reduce_scatter | solution.py:257
  386.6 16.6 %all-to-all-start.7 = ((bf16[8,160,192]{2,1,0:T(8,128)(2,1)}), bf16[8,160,192]{2,1,0:T(8,128)(2,1)}, u32[]{:S(2)}, u32[]{:S(2)}) async-start(bf16[8,160,192]{2,1,0:T(8,128)(2,1)} %bitcast.149), calls=%async_computation.7 | async-start | bytes 1310720 | tf_op jit(solution)/shard_map/all_to_all | solution.py:216
  403.2 23.0 %all-to-all-start.5 = ((bf16[8,64,1280]{2,1,0:T(8,128)(2,1)}), bf16[8,64,1280]{2,1,0:T(8,128)(2,1)}, u32[]{:S(2)}, u32[]{:S(2)}) async-start(bf16[8,64,1280]{2,1,0:T(8,128)(2,1)} %bitcast.157), calls=%async_computation.5 | async-start | bytes 2621440 | tf_op jit(solution)/shard_map/all_to_all | solution.py:60
  409.3 67.0 %reduce-scatter.22.cloned.1.call-start = ((), (), s32[]{:S(2)}) async-start(), calls=%async_computation.22 | async-start | bytes 696320
  409.9 129.3 %reduce-scatter.20.cloned.1.call-start = ((), (), s32[]{:S(2)}) async-start(), calls=%async_computation.21 | async-start | bytes 835584
  431.2 23.9 %all-to-all-start.6 = ((bf16[8,64,1280]{2,1,0:T(8,128)(2,1)}), bf16[8,64,1280]{2,1,0:T(8,128)(2,1)}, u32[]{:S(2)}, u32[]{:S(2)}) async-start(bf16[8,64,1280]{2,1,0:T(8,128)(2,1)} %broadcast_in_dim.32), calls=%async_computation.6 | async-start | bytes 2621440 | tf_op jit(solution)/shard_map/all_to_all | solution.py:22
  436.4 166.4 %reduce-scatter.18.cloned.1.call-start = ((), (), s32[]{:S(2)}) async-start(), calls=%async_computation.20 | async-start | bytes 1392640
  451.2 218.6 %reduce-scatter.16.cloned.1.call-start = ((), (), s32[]{:S(2)}) async-start(), calls=%async_computation.19 | async-start | bytes 3481600
  (28 other events, 71.3 us)
Sparse Core Ops, SparseCore 0:
  16.4 95.9 all-reduce.1
  119.8 70.9 all-gather.3
  263.4 70.1 all-gather.5
  335.8 61.6 reduce-scatter.13
  412.1 64.1 reduce-scatter.21
  478.5 60.5 reduce-scatter.19
  541.5 61.2 reduce-scatter.17
  605.3 64.4 reduce-scatter.15
where the time goes:
time: 692 us; the launch traced here: 680 us
  waiting for transfers between devices  356 us (51%)
  local copies, waits for them, and re-layouts  147 us (21%)
  starting transfers between devices  56.1 us (8%)
  other arithmetic  45.7 us (7%)
  matrix products  42.4 us (6%)
  between operations  19 us (3%)
  blocking collectives  13.1 us (2%)
    unnamed x12, waiting for transfers between devices  190 us
    psum x1, waiting for transfers between devices, local(): hidden = tokens.astype(jnp.float32) + lax.psum(mixed, 'mp')  96.1 us
    unnamed x90, local copies, waits for them, and re-layouts  44.9 us
    all_gather x1, waiting for transfers between devices, gather_packed(): lines, at, done = (lax.all_gather(vector, axis), 0, [])  39.3 us
    all_to_all x3, starting transfers between devices, local(): lax.all_to_all(for_sending(column_grads), 'mp', split_axis=0, concat_axis...  18.7 us
    reshape x3, local copies, waits for them, and re-layouts, gather_packed(): pieces = lines[:, at:at + a.size].reshape(-1, *a.shape)  13.9 us
  transfers between devices with their start and end apart: 17, of which 12 were waited for; matrix products, arithmetic and copies ran while one was open for 27% of the time, Pallas kernels for 0%

commit v1 on v0

v1 whole, which is shorter than its diff:
```python
import jax
import jax.numpy as jnp
from jax import lax
from jax.experimental import pallas as pl
from jax.experimental.pallas import tpu as pltpu
from jax.sharding import PartitionSpec as P

F32, BF16 = jnp.float32, jnp.bfloat16
MESH = pl.DeviceIdType.MESH

R, D, FB, HB = 512, 1280, 640, 160
DP, MP, PATCH = 16, 8, 32
WIDTHS = (1536, 1152, 1280)
CB = tuple(w // MP for w in WIDTHS)
PB = tuple(w // DP for w in WIDTHS)
BASE = (0, 1536, 2688)
OFF = (0, 192, 336)
HOFF = (0, 96, 176)
CH, CBS = 3968, 496
BLK = R // MP
DB = D // DP

slope_coef = 0.7978845608028654
cubic_coef = 0.044715


def smooth(value):
    return 0.5 * value * (1.0 + jnp.tanh(slope_coef * (value + cubic_coef * value * value * value)))


def smooth_slope(value):
    square = value * value
    tangent = jnp.tanh(slope_coef * (value + cubic_coef * value * square))
    return 0.5 * (1.0 + tangent) + 0.5 * value * (1.0 - tangent * tangent) * slope_coef * (
        1.0 + 3.0 * cubic_coef * square
    )


def nn(a, b):
    return lax.dot_general(a, b, (((1,), (0,)), ((), ())), preferred_element_type=F32)


def nt(a, b):
    return lax.dot_general(a, b, (((1,), (1,)), ((), ())), preferred_element_type=F32)


def eye(n):
    return (
        lax.broadcasted_iota(jnp.int32, (n, n), 0) == lax.broadcasted_iota(jnp.int32, (n, n), 1)
    ).astype(F32).astype(BF16)


def flipped(block):
    return nt(eye(block.shape[1]), block).astype(BF16)


def remote(src, dst, send, recv, where):
    return pltpu.make_async_remote_copy(
        src_ref=src, dst_ref=dst, send_sem=send, recv_sem=recv, device_id=where, device_id_type=MESH
    )


def aligned(value, n):
    return pl.multiple_of(value, n)


def kernel(
    lags, slots, tok, ng, ww, nw, fg, ai, h0, h1, h2, t0, t1, t2,
    out_w, out_n, out_a, out_h,
    first, wide, active, part, rs1, final, normal, inverse,
    headt, before, lift, sp, rs2, stu, tsend, trecv, tgt, stats, statr,
    slo, inner, part2, rs3, thr, finalt,
    hf32, hsend, hcore, hmid, hrecv, asend, acore, amid, arecv,
    nsend, ncore, nmid, nrecv, wsend, wcore, wmid, wrecv,
    row_s, row_r, tea_s, tea_r, stu_s, stu_r, sta_s, sta_r, slo_s, slo_r,
    cor_s, cor_r, dp_s, dp_r,
):
    d = lax.axis_index("dp")
    m = lax.axis_index("mp")
    core = lax.rem(d, 2)
    half = d // 2
    heads = (h0, h1, h2)
    teachers = (t0, t1, t2)
    partner = half * 2 + (1 - core)

    def mate(i):
        return lax.rem(m + i, MP)

    def greet(i, _):
        pl.semaphore_signal(barrier, inc=1, device_id={"mp": mate(i)}, device_id_type=MESH)
        return _

    def greet_dp(i, _):
        pl.semaphore_signal(barrier, inc=1, device_id={"dp": lax.rem(d + i, DP)}, device_id_type=MESH)
        return _

    barrier = pltpu.get_barrier_semaphore()
    lax.fori_loop(1, MP, greet, 0)
    lax.fori_loop(1, DP, greet_dp, 0)
    pl.semaphore_wait(barrier, MP - 1 + DP - 1)

    def forward(i, _):
        q = lax.rem(m // 2 + 1 + i, 4)
        rows = pl.ds(aligned(q * 128, 128), 128)
        value = tok[rows, :].astype(F32)
        centre = value - jnp.mean(value, axis=-1, keepdims=True)
        inv = lax.rsqrt(jnp.mean(centre * centre, axis=-1, keepdims=True) + 1e-06)
        first[rows, :] = (centre * inv * ng[...]).astype(BF16)
        w = nn(first[rows, :], ww[...])
        wide[rows, :] = w
        active[rows, :] = smooth(w).astype(BF16)
        part[rows, :] = nn(active[rows, :], nw[...]).astype(BF16)
        for k in range(2):
            p = q * 2 + k

            @pl.when(p != m)
            def _send():
                mine = part.at[pl.ds(aligned(p * BLK, BLK), BLK)]
                remote(mine, rs1.at[m], row_s.at[0, p], row_r.at[0, m], {"mp": p}).start()

        return _

    lax.fori_loop(0, 4, forward, 0)

    def slopes_of(ref, n):
        def body(i, _):
            rows = pl.ds(aligned(i * 32, 32), 32)
            ref[rows, :] = smooth_slope(ref[rows, :])
            return _

        lax.fori_loop(0, n // 32, body, 0)

    def grid(shape, dim):
        return lax.broadcasted_iota(jnp.int32, shape, dim)

    def ones_where(condition):
        return condition.astype(F32).astype(BF16)

    slot = slots[...].reshape(1, DP * DP)
    spread_out = ones_where(grid((DP * DP, R), 0) == d * DP + grid((DP * DP, R), 1) // PATCH)
    own_slot = nn(jnp.broadcast_to(slot, (16, DP * DP)).astype(F32).astype(BF16), spread_out)[0:1]
    goes = own_slot.astype(jnp.int32) // DP
    same_patch = lax.rem(grid((R, R), 0), PATCH) == lax.rem(grid((R, R), 1), PATCH)
    chosen = ones_where((goes == grid((R, R), 0) // PATCH) & same_patch)
    for t in range(3):
        late = (lags[t] - 1).astype(F32)
        stale = teachers[t][0].astype(F32) * (1.0 - late) + teachers[t][1].astype(F32) * late
        tsend[:, 256 * t : 256 * t + CB[t]] = nt(chosen, stale.astype(BF16)).astype(BF16)

    def images_of(j):
        return pl.ds(aligned(j * PATCH, PATCH), PATCH)

    def teach(i, _):
        j = lax.rem(d + i, DP)
        remote(tsend.at[images_of(j)], trecv.at[images_of(d)], tea_s.at[j], tea_r.at[d], {"dp": j}).start()
        return _

    lax.fori_loop(1, DP, teach, 0)
    trecv[images_of(d), :] = tsend[images_of(d), :]

    slopes_of(wide, R)
    for t in range(3):
        def head_block(i, _, t=t):
            at = aligned(i * 128, 128)
            headt[pl.ds(aligned(BASE[t] + at, 128), 128), :] = flipped(heads[t][:, pl.ds(at, 128)])
            return _

        lax.fori_loop(0, WIDTHS[t] // 128, head_block, 0)

    own_rows = pl.ds(aligned(m * BLK, BLK), BLK)

    def gathered(buffer, which, received):
        total = buffer[own_rows, :].astype(F32)
        for i in range(1, MP):
            p = mate(i)
            remote(received.at[p], received.at[p], row_s.at[which, p], row_r.at[which, p], {"mp": p}).wait_recv()
            total = total + received[p].astype(F32)
        return total

    def spread(buffer, which):
        def body(i, _):
            p = mate(i)
            remote(buffer.at[own_rows], buffer.at[own_rows], row_s.at[which, p], row_r.at[which, m], {"mp": p}).start()
            return _

        lax.fori_loop(1, MP, body, 0)

    def arrived(buffer, which):
        def body(i, _):
            p = mate(i)
            there = buffer.at[pl.ds(aligned(p * BLK, BLK), BLK)]
            remote(there, there, row_s.at[which, p], row_r.at[which, p], {"mp": p}).wait_recv()
            return _

        lax.fori_loop(1, MP, body, 0)

    hidden = tok[own_rows, :].astype(F32) + gathered(part, 0, rs1)
    centre = hidden - jnp.mean(hidden, axis=-1, keepdims=True)
    inv = lax.rsqrt(jnp.mean(centre * centre, axis=-1, keepdims=True) + 1e-06)
    normal[...] = centre * inv
    inverse[...] = jnp.broadcast_to(inv, (BLK, 128))
    final[own_rows, :] = (normal[...] * fg[...]).astype(BF16)
    spread(final, 1)

    def landed(i, _):
        j = lax.rem(d + i, DP)
        remote(tsend.at[images_of(j)], trecv.at[images_of(j)], tea_s.at[j], tea_r.at[j], {"dp": j}).wait_recv()
        return _

    lax.fori_loop(1, DP, landed, 0)

    holds = ones_where(slot == d * DP + grid((R, DP * DP), 0) // PATCH)
    group = ones_where(grid((R, DP * DP), 1) // DP == grid((R, DP * DP), 0) // PATCH)
    placing = jnp.where(same_patch, nt(group, holds), 0.0).astype(BF16)
    for t in range(3):
        block = flipped(trecv[:, 256 * t : 256 * t + CB[t]])
        tgt[OFF[t] : OFF[t] + CB[t], :] = nn(block, placing).astype(BF16)

    arrived(final, 1)

    for t in range(3):
        units = slice(t * HB, (t + 1) * HB)
        b = nt(ai[t], final[...])
        before[units, :] = b
        lift[units, :] = smooth(b).astype(BF16)

        def student(i, _, t=t, units=units):
            p = mate(i)
            rows = pl.ds(aligned(BASE[t] + p * CB[t], 16), CB[t])
            sp[rows, :] = nn(headt[rows, :], lift[units, :]).astype(BF16)

            @pl.when(p != m)
            def _send():
                there = rs2.at[m, OFF[t] : OFF[t] + CB[t]]
                remote(sp.at[rows], there, stu_s.at[t, p], stu_r.at[t, m], {"mp": p}).start()

            return _

        lax.fori_loop(1, MP + 1, student, 0)

    slopes_of(before, 3 * HB)

    def final_block(i, _):
        at = aligned(i * 128, 128)
        finalt[pl.ds(at, 128), :] = flipped(final[:, pl.ds(at, 128)])
        return _

    lax.fori_loop(0, D // 128, final_block, 0)

    def gather_student(t):
        mine = slice(OFF[t], OFF[t] + CB[t])
        stu[mine, :] = sp[pl.ds(aligned(BASE[t] + m * CB[t], 16), CB[t]), :].astype(F32)

        def body(i, _):
            p = mate(i)
            here = rs2.at[p, mine]
            remote(here, here, stu_s.at[t, p], stu_r.at[t, p], {"mp": p}).wait_recv()
            stu[mine, :] += rs2[p, mine].astype(F32)
            return _

        lax.fori_loop(1, MP, body, 0)
        y = stu[mine, :]
        f = tgt[mine, :].astype(F32)
        stats[t, 0:1, :] = jnp.sum(y * f, axis=0, keepdims=True)
        stats[t, 1:2, :] = jnp.sum(y * y, axis=0, keepdims=True)
        stats[t, 2:3, :] = jnp.sum(f * f, axis=0, keepdims=True)
        stats[t, 3:8, :] = jnp.zeros((5, R), F32)

        def send(i, _):
            p = mate(i)
            remote(stats.at[t], statr.at[t, m], sta_s.at[t, p], sta_r.at[t, m], {"mp": p}).start()
            return _

        lax.fori_loop(1, MP, send, 0)

    def slope(t):
        mine = slice(OFF[t], OFF[t] + CB[t])
        total = stats[t]
        for i in range(1, MP):
            p = mate(i)
            remote(stats.at[t], statr.at[t, p], sta_s.at[t, p], sta_r.at[t, p], {"mp": p}).wait_recv()
            total = total + statr[t, p]
        square_student = total[1:2] + 1e-06
        joint = lax.rsqrt(square_student * (total[2:3] + 1e-06))
        scale = total[0:1] * joint / square_student
        rows = pl.ds(aligned(BASE[t] + m * CB[t], 16), CB[t])
        slo[rows, :] = (scale * stu[mine, :] - joint * tgt[mine, :].astype(F32)).astype(BF16)

        def send(i, _):
            p = mate(i)
            remote(slo.at[rows], slo.at[rows], slo_s.at[t, p], slo_r.at[t, m], {"mp": p}).start()
            return _

        lax.fori_loop(1, MP, send, 0)

    gather_student(0)
    gather_student(1)
    slope(0)
    gather_student(2)
    slope(1)
    slope(2)

    for t in range(3):
        def slopes_in(i, _, t=t):
            p = mate(i)
            there = slo.at[pl.ds(aligned(BASE[t] + p * CB[t], 16), CB[t])]
            remote(there, there, slo_s.at[t, p], slo_r.at[t, p], {"mp": p}).wait_recv()
            return _

        lax.fori_loop(1, MP, slopes_in, 0)
        units = slice(t * HB, (t + 1) * HB)
        back = nn(heads[t][...], slo[BASE[t] : BASE[t] + WIDTHS[t], :])
        inner[units, :] = (back * before[units, :]).astype(BF16)

    def up(i, _):
        q = lax.rem(m // 2 + 1 + i, 4)
        rows = pl.ds(aligned(q * 128, 128), 128)
        part2[rows, :] = nn(flipped(inner[:, rows]), ai[...].reshape(3 * HB, D)).astype(BF16)
        for k in range(2):
            p = q * 2 + k

            @pl.when(p != m)
            def _send():
                mine = part2.at[pl.ds(aligned(p * BLK, BLK), BLK)]
                remote(mine, rs3.at[m], row_s.at[2, p], row_r.at[2, m], {"mp": p}).start()

        return _

    lax.fori_loop(0, 4, up, 0)

    def to_partner(which, send, received):
        def body(k, _):
            j = k * 2 + (1 - core)
            remote(send.at[j], received.at[k], cor_s.at[which, k], cor_r.at[which, k], {"dp": partner}).start()
            return _

        lax.fori_loop(0, 8, body, 0)

    def onward(which, send, received, mid, last):
        def body(i, _):
            k = lax.rem(half + i, 8)
            remote(send.at[k], received.at[k], cor_s.at[which, k], cor_r.at[which, k], {"dp": partner}).wait_recv()
            mid[k] = (send[k * 2 + core].astype(F32) + received[k].astype(F32)).astype(BF16)

            @pl.when(k != half)
            def _send():
                remote(mid.at[k], last.at[half], dp_s.at[which, k], dp_r.at[which, half], {"dp": k * 2 + core}).start()

            return _

        lax.fori_loop(1, 9, body, 0)

    def reduced(which, mid, last, out):
        out[...] = mid[half].astype(F32)

        def body(i, _):
            k = lax.rem(half + i, 8)
            remote(mid.at[k], last.at[k], dp_s.at[which, k], dp_r.at[which, k], {"dp": k * 2 + core}).wait_recv()
            out[...] += last[k].astype(F32)
            return _

        lax.fori_loop(1, 8, body, 0)

    for t in range(3):
        def head_grad(i, _, t=t):
            at = aligned(i * 128, 128)
            rows = pl.ds(aligned(BASE[t] + at, 128), 128)
            hf32[pl.ds(at, 128), :] = nt(slo[rows, :], lift[t * HB : (t + 1) * HB, :])
            return _

        lax.fori_loop(0, WIDTHS[t] // 128, head_grad, 0)

        def head_piece(j, _, t=t):
            rows = pl.ds(aligned(j * PB[t], 8), PB[t])
            hsend[j, HOFF[t] : HOFF[t] + PB[t], :] = hf32[rows, :].astype(BF16)
            return _

        lax.fori_loop(0, DP, head_piece, 0)
    to_partner(0, hsend, hcore)

    def adaptor_grad(j, _):
        asend[j] = nt(finalt[pl.ds(aligned(j * DB, 16), DB), :], inner[...]).astype(BF16)
        return _

    lax.fori_loop(0, DP, adaptor_grad, 0)
    to_partner(1, asend, acore)
    onward(0, hsend, hcore, hmid, hrecv)
    onward(1, asend, acore, amid, arecv)

    upstream = gathered(part2, 2, rs3)
    scaled = upstream * fg[...]
    hat = normal[...]
    through = inverse[:, 0:1] * (
        scaled
        - jnp.mean(scaled, axis=-1, keepdims=True)
        - hat * jnp.mean(scaled * hat, axis=-1, keepdims=True)
    )
    thr[own_rows, :] = through.astype(BF16)
    spread(thr, 3)
    arrived(thr, 3)

    def flip_all(src):
        def body(i, _):
            at = aligned(i * 128, 128)
            finalt[pl.ds(at, 128), :] = flipped(src[:, pl.ds(at, 128)])
            return _

        lax.fori_loop(0, D // 128, body, 0)

    flip_all(thr)

    def narrow_grad(j, _):
        nsend[j] = nn(finalt[pl.ds(aligned(j * DB, 16), DB), :], active[...]).astype(BF16)
        return _

    lax.fori_loop(0, DP, narrow_grad, 0)
    to_partner(2, nsend, ncore)
    flip_all(first)

    def backward(i, _):
        rows = pl.ds(aligned(i * 128, 128), 128)
        active[rows, :] = (nt(thr[rows, :], nw[...]) * wide[rows, :]).astype(BF16)
        return _

    lax.fori_loop(0, 4, backward, 0)
    onward(2, nsend, ncore, nmid, nrecv)

    def widen_grad(j, _):
        wsend[j] = nn(finalt[pl.ds(aligned(j * DB, 16), DB), :], active[...]).astype(BF16)
        return _

    lax.fori_loop(0, DP, widen_grad, 0)
    to_partner(3, wsend, wcore)
    onward(3, wsend, wcore, wmid, wrecv)
    reduced(0, hmid, hrecv, out_h)
    reduced(1, amid, arecv, out_a)
    reduced(2, nmid, nrecv, out_n)
    reduced(3, wmid, wrecv, out_w)

    def sent_dp(i, _):
        j = lax.rem(d + i, DP)
        remote(tsend.at[images_of(j)], trecv.at[images_of(d)], tea_s.at[j], tea_r.at[d], {"dp": j}).wait_send()
        return _

    lax.fori_loop(1, DP, sent_dp, 0)

    def sent_mp(i, _):
        p = mate(i)
        where = {"mp": p}
        for which, (src, dst) in enumerate(((part, rs1), (final, rs1), (part2, rs3), (thr, rs3))):
            remote(src.at[own_rows], dst.at[m], row_s.at[which, p], row_r.at[which, m], where).wait_send()
        for t in range(3):
            rows = pl.ds(aligned(BASE[t] + p * CB[t], 16), CB[t])
            there = rs2.at[m, OFF[t] : OFF[t] + CB[t]]
            remote(sp.at[rows], there, stu_s.at[t, p], stu_r.at[t, m], where).wait_send()
            remote(stats.at[t], statr.at[t, m], sta_s.at[t, p], sta_r.at[t, m], where).wait_send()
            remote(slo.at[rows], slo.at[rows], slo_s.at[t, p], slo_r.at[t, m], where).wait_send()
        return _

    lax.fori_loop(1, MP, sent_mp, 0)
    reductions = (
        (hsend, hcore, hmid, hrecv),
        (asend, acore, amid, arecv),
        (nsend, ncore, nmid, nrecv),
        (wsend, wcore, wmid, wrecv),
    )

    def sent_core(k, _):
        for which, (send, received, mid, last) in enumerate(reductions):
            remote(send.at[k], received.at[k], cor_s.at[which, k], cor_r.at[which, k], {"dp": partner}).wait_send()
        return _

    lax.fori_loop(0, 8, sent_core, 0)

    def sent_chip(i, _):
        k = lax.rem(half + i, 8)
        for which, (send, received, mid, last) in enumerate(reductions):
            remote(mid.at[k], last.at[half], dp_s.at[which, k], dp_r.at[which, half], {"dp": k * 2 + core}).wait_send()
        return _

    lax.fori_loop(1, 8, sent_chip, 0)


def local(
    tokens, norm_gain, widen_weight, narrow_weight, final_gain, adaptor_in,
    head_dino, head_siglip, head_sam, teacher_dino, teacher_siglip, teacher_sam,
    step_lags, owner_slot,
):
    vmem = pl.BlockSpec(memory_space=pltpu.VMEM)

    def reduction(rows, columns):
        return [
            pltpu.VMEM((DP, rows, columns), BF16),
            pltpu.VMEM((8, rows, columns), BF16),
            pltpu.VMEM((8, rows, columns), BF16),
            pltpu.VMEM((8, rows, columns), BF16),
        ]

    dma = pltpu.SemaphoreType.DMA
    w, n, a, h = pl.pallas_call(
        kernel,
        out_shape=(
            jax.ShapeDtypeStruct((DB, FB), F32),
            jax.ShapeDtypeStruct((DB, FB), F32),
            jax.ShapeDtypeStruct((DB, 3 * HB), F32),
            jax.ShapeDtypeStruct((256, HB), F32),
        ),
        in_specs=[pl.BlockSpec(memory_space=pltpu.SMEM)] + [vmem] * 13,
        out_specs=(vmem,) * 4,
        scratch_shapes=[
            pltpu.VMEM((R, D), BF16),
            pltpu.VMEM((R, FB), F32),
            pltpu.VMEM((R, FB), BF16),
            pltpu.VMEM((R, D), BF16),
            pltpu.VMEM((MP, BLK, D), BF16),
            pltpu.VMEM((R, D), BF16),
            pltpu.VMEM((BLK, D), F32),
            pltpu.VMEM((BLK, 128), F32),
            pltpu.VMEM((CH, HB), BF16),
            pltpu.VMEM((3 * HB, R), F32),
            pltpu.VMEM((3 * HB, R), BF16),
            pltpu.VMEM((CH, R), BF16),
            pltpu.VMEM((MP, CBS, R), BF16),
            pltpu.VMEM((CBS, R), F32),
            pltpu.VMEM((R, 768), BF16),
            pltpu.VMEM((R, 768), BF16),
            pltpu.VMEM((CBS, R), BF16),
            pltpu.VMEM((3, 8, R), F32),
            pltpu.VMEM((3, MP, 8, R), F32),
            pltpu.VMEM((CH, R), BF16),
            pltpu.VMEM((3 * HB, R), BF16),
            pltpu.VMEM((R, D), BF16),
            pltpu.VMEM((MP, BLK, D), BF16),
            pltpu.VMEM((R, D), BF16),
            pltpu.VMEM((D, R), BF16),
            pltpu.VMEM((1536, HB), F32),
            *reduction(256, HB),
            *reduction(DB, 3 * HB),
            *reduction(DB, FB),
            *reduction(DB, FB),
            dma((4, MP)), dma((4, MP)),
            dma((DP,)), dma((DP,)),
            dma((3, MP)), dma((3, MP)),
            dma((3, MP)), dma((3, MP)),
            dma((3, MP)), dma((3, MP)),
            dma((4, 8)), dma((4, 8)),
            dma((4, 8)), dma((4, 8)),
        ],
        compiler_params=pltpu.CompilerParams(
            collective_id=0, has_side_effects=True, vmem_limit_bytes=66_000_000
        ),
        name="step",
    )(
        step_lags, owner_slot[None], tokens, norm_gain[None], widen_weight, narrow_weight, final_gain[None],
        adaptor_in.transpose(0, 2, 1), head_dino, head_siglip, head_sam,
        teacher_dino.transpose(0, 2, 1), teacher_siglip.transpose(0, 2, 1), teacher_sam.transpose(0, 2, 1),
    )
    return (
        w.T,
        n.T,
        a.reshape(DB, 3, HB).transpose(1, 0, 2),
        h[0:96].T,
        h[96:168].T,
        h[176:256].T,
    )


def solution(mesh):
    placed = (
        P("dp", None),
        P(),
        P(None, "mp"),
        P("mp", None),
        P(),
        P(None, None, "mp"),
        P("mp", None),
        P("mp", None),
        P("mp", None),
        P(None, "dp", "mp"),
        P(None, "dp", "mp"),
        P(None, "dp", "mp"),
        P(),
        P(),
    )
    return jax.shard_map(
        local,
        mesh=mesh,
        in_specs=placed,
        out_specs=(
            P("mp", "dp"),
            P("mp", "dp"),
            P(None, "dp", "mp"),
            P("mp", "dp"),
            P("mp", "dp"),
            P("mp", "dp"),
        ),
        check_vma=False,
    )
```

time: 692 us -> 249 us (0.36); the launches traced: 680 us -> 249 us
  waiting for transfers between devices: 356 us -> 0 us
  Pallas kernels: 0 us -> 238 us
  local copies, waits for them, and re-layouts: 147 us -> 10.7 us
  starting transfers between devices: 56.1 us -> 0 us
  other arithmetic: 45.7 us -> 0 us
  matrix products: 42.4 us -> 0 us
  between operations: 19 us -> 0.67 us
  blocking collectives: 13.1 us -> 0 us
    pallas_call x0 -> x1, Pallas kernels: none -> 238 us  [local(): pl.pallas_call(kernel, out_shape=(jax.ShapeDtypeStruct((DB, FB), F32), ja...]
    unnamed x12 -> x0, waiting for transfers between devices: 190 us -> none
    psum x1 -> x0, waiting for transfers between devices: 96.1 us -> none  [local(): hidden = tokens.astype(jnp.float32) + lax.psum(mixed, 'mp')]
    all_to_all x9 -> x0, starting transfers between devices: 55.3 us -> none  [the longest x3 18.7 us: local(): lax.all_to_all(for_sending(column_grads), 'mp', split_axis=0, concat_axis...]
    dot_general x15 -> x0, matrix products: 41.6 us -> none  [the longest x3 7.94 us: local(): jnp.einsum('rh,rc->hc', whole_lifted[index], local_slopes[index], preferr...]
    unnamed x90 -> x9, local copies, waits for them, and re-layouts: 44.9 us -> 3.69 us
    all_gather x2 -> x0, waiting for transfers between devices: 39.3 us -> none  [the longest x1 39.3 us: gather_packed(): lines, at, done = (lax.all_gather(vector, axis), 0, [])]
    all_to_all x9 -> x0, waiting for transfers between devices: 31.3 us -> none  [the longest x1 13.2 us: sent_and_summed(): lax.all_to_all(pieces, axis, split_axis=0, concat_axis=0, tiled=True)]
  transfers between devices with their start and end apart: 17 -> 0, of which waited for: 12 -> 0; matrix products, arithmetic and copies ran while one was open for 27% -> 0% of each run, Pallas kernels for 0% -> 0%
where the time goes in v1:
time: 249 us
  Pallas kernels  238 us (96%)
  local copies, waits for them, and re-layouts  10.7 us (4%)
    pallas_call x1, Pallas kernels, local(): pl.pallas_call(kernel, out_shape=(jax.ShapeDtypeStruct((DB, FB), F32), ja...  238 us

profile of v1, /device:TPU:24, one launch (start us, length us, event | category | flops | bytes accessed | tf_op | source)
XLA Modules:
  0.0 249.0 jit_solution(10246590561909859904)
XLA Ops:
  0.6 1.3 broadcast_in_dim.10.ng
  1.9 1.3 broadcast_in_dim.11.fg
  3.2 237.7 %step.1 = (f32[80,640]{1,0:T(8,128)}, f32[80,640]{1,0:T(8,128)}, f32[80,480]{1,0:T(8,128)}, f32[256,160]{1,0:T(8,128)}) custom-call(s32[3]{0:T(128)} %lags.1, s32[1,256]{1,0:T(1,128)} %bitcast.23, bf16[512,1280]{1,0:T(8,128)(2,1)} %tok.1, f32[1,1280]{1,0:T(1,128)} %broadcast_in_dim.10.ng, bf16[1280,640]{1,0:T(8,128)(2,1)} %ww.1, bf16[640,1280]{1,0:T(8,128)(2,1)} %nw.1, ...), custom_call_target="tpu_custom_call" | custom-call | tf_op jit(solution)/shard_map/step/pallas_call | solution.py:500
  240.9 0.0 copy-start.1
  240.9 0.0 copy-start
  240.9 1.6 slice_bitcast_fusion.2
  242.5 0.9 slice_bitcast_fusion.1
  243.4 0.9 slice_bitcast_fusion
  244.3 0.7 copy.25
  245.0 0.7 copy.26
  245.8 1.0 copy.23
  246.8 0.9 copy.24
  247.7 0.0 copy-done.1
  247.7 0.7 copy.29
  248.3 0.0 copy-done
  248.3 0.7 copy.30
Async XLA Ops:
  240.9 6.8 %copy-start.1 = (f32[80,640]{1,0:T(8,128)S(1)}, f32[80,640]{1,0:T(8,128)}, u32[]{:S(2)}) copy-start(f32[80,640]{1,0:T(8,128)} %get-tuple-element.10) | copy-start | bytes 614404
  240.9 7.4 %copy-start = (f32[80,640]{1,0:T(8,128)S(1)}, f32[80,640]{1,0:T(8,128)}, u32[]{:S(2)}) copy-start(f32[80,640]{1,0:T(8,128)} %get-tuple-element.11) | copy-start | bytes 614404

commit v2 on v1

--- a/solution.py
+++ b/solution.py
@@ -65,12 +65,20 @@
 
 
 def kernel(
-    lags, slots, tok, ng, ww, nw, fg, ai, h0, h1, h2, t0, t1, t2,
-    out_w, out_n, out_a, out_h,
+    lags, slots, ng, fg, *refs,
+):
+    outside, refs = refs[:10], refs[10:]
+    outputs, inside, load_sem, refs = refs[:6], refs[6:16], refs[16], refs[17:]
+    step(lags, slots, ng, fg, outside, load_sem, *inside, *outputs, *refs)
+
+
+def step(
+    lags, slots, ng, fg, outside, load_sem, tok, ww, nw, t0, t1, t2, ai, h0, h1, h2,
+    out_w, out_n, out_a, out_d, out_g, out_s,
     first, wide, active, part, rs1, final, normal, inverse,
     headt, before, lift, sp, rs2, stu, tsend, trecv, tgt, stats, statr,
-    slo, inner, part2, rs3, thr, finalt,
-    hf32, hsend, hcore, hmid, hrecv, asend, acore, amid, arecv,
+    slo, inner, part2, rs3, thr, finalt, firstt,
+    hf32, hacc, aacc, hsend, hcore, hmid, hrecv, asend, acore, amid, arecv,
     nsend, ncore, nmid, nrecv, wsend, wcore, wmid, wrecv,
     row_s, row_r, tea_s, tea_r, stu_s, stu_r, sta_s, sta_r, slo_s, slo_r,
     cor_s, cor_r, dp_s, dp_r,
@@ -79,6 +87,10 @@
     m = lax.axis_index("mp")
     core = lax.rem(d, 2)
     half = d // 2
+    loads = [
+        pltpu.make_async_copy(src, dst, load_sem.at[k])
+        for k, (src, dst) in enumerate(zip(outside, (tok, ww, nw, t0, t1, t2, ai, h0, h1, h2)))
+    ]
     heads = (h0, h1, h2)
     teachers = (t0, t1, t2)
     partner = half * 2 + (1 - core)
@@ -97,15 +109,26 @@
     barrier = pltpu.get_barrier_semaphore()
     lax.fori_loop(1, MP, greet, 0)
     lax.fori_loop(1, DP, greet_dp, 0)
-    pl.semaphore_wait(barrier, MP - 1 + DP - 1)
-
-    def forward(i, _):
-        q = lax.rem(m // 2 + 1 + i, 4)
-        rows = pl.ds(aligned(q * 128, 128), 128)
+    for load in loads:
+        load.start()
+    loads[0].wait()
+
+    def normalized(i, _):
+        rows = pl.ds(aligned(i * 128, 128), 128)
         value = tok[rows, :].astype(F32)
         centre = value - jnp.mean(value, axis=-1, keepdims=True)
         inv = lax.rsqrt(jnp.mean(centre * centre, axis=-1, keepdims=True) + 1e-06)
         first[rows, :] = (centre * inv * ng[...]).astype(BF16)
+        return _
+
+    lax.fori_loop(0, 4, normalized, 0)
+    loads[1].wait()
+    loads[2].wait()
+    pl.semaphore_wait(barrier, MP - 1 + DP - 1)
+
+    def forward(i, _):
+        q = lax.rem(m // 2 + 1 + i, 4)
+        rows = pl.ds(aligned(q * 128, 128), 128)
         w = nn(first[rows, :], ww[...])
         wide[rows, :] = w
         active[rows, :] = smooth(w).astype(BF16)
@@ -136,6 +159,8 @@
     def ones_where(condition):
         return condition.astype(F32).astype(BF16)
 
+    for load in loads[3:]:
+        load.wait()
     slot = slots[...].reshape(1, DP * DP)
     spread_out = ones_where(grid((DP * DP, R), 0) == d * DP + grid((DP * DP, R), 1) // PATCH)
     own_slot = nn(jnp.broadcast_to(slot, (16, DP * DP)).astype(F32).astype(BF16), spread_out)[0:1]
@@ -240,12 +265,16 @@
 
     slopes_of(before, 3 * HB)
 
-    def final_block(i, _):
-        at = aligned(i * 128, 128)
-        finalt[pl.ds(at, 128), :] = flipped(final[:, pl.ds(at, 128)])
-        return _
-
-    lax.fori_loop(0, D // 128, final_block, 0)
+    def flip_all(src, dst):
+        def body(i, _):
+            at = aligned(i * 128, 128)
+            dst[pl.ds(at, 128), :] = flipped(src[:, pl.ds(at, 128)])
+            return _
+
+        lax.fori_loop(0, D // 128, body, 0)
+
+    flip_all(final, finalt)
+    flip_all(first, firstt)
 
     def gather_student(t):
         mine = slice(OFF[t], OFF[t] + CB[t])
@@ -286,28 +315,58 @@
         rows = pl.ds(aligned(BASE[t] + m * CB[t], 16), CB[t])
         slo[rows, :] = (scale * stu[mine, :] - joint * tgt[mine, :].astype(F32)).astype(BF16)
 
-        def send(i, _):
-            p = mate(i)
-            remote(slo.at[rows], slo.at[rows], slo_s.at[t, p], slo_r.at[t, m], {"mp": p}).start()
-            return _
-
-        lax.fori_loop(1, MP, send, 0)
+        pass_on(t, m, 0, place(pair, ring + 1))
+        pass_on(t, m, 1, place(pair, ring + 3))
+        pass_on(t, m, 2, place(1 - pair, ring))
+
+    pair, ring = m // 4, lax.rem(m, 4)
+    turn = (1, 3, 3)
+
+    def place(a, b):
+        return a * 4 + lax.rem(b, 4)
+
+    def slope_copy(t, owner, k, to):
+        block = slo.at[pl.ds(aligned(BASE[t] + owner * CB[t], 16), CB[t])]
+        return remote(block, block, slo_s.at[t, k], slo_r.at[t, owner], {"mp": to})
+
+    def pass_on(t, owner, k, to):
+        slope_copy(t, owner, k, to).start()
+
+    def got(t, owner):
+        slope_copy(t, owner, 0, owner).wait_recv()
+
+    def first_relay(t):
+        owner = place(pair, ring + 4 - turn[t])
+        got(t, owner)
+        pass_on(t, owner, 3, place(pair, ring + turn[t]))
+        owner = place(1 - pair, ring)
+        got(t, owner)
+        pass_on(t, owner, 4, place(pair, ring + turn[t]))
+        pass_on(t, owner, 5, place(pair, ring + 4 - turn[t]))
+
+    def second_relay(t):
+        owner = place(pair, ring + 2)
+        got(t, owner)
+        pass_on(t, owner, 6, place(1 - pair, ring))
 
     gather_student(0)
     gather_student(1)
     slope(0)
     gather_student(2)
     slope(1)
+    first_relay(0)
     slope(2)
-
-    for t in range(3):
-        def slopes_in(i, _, t=t):
-            p = mate(i)
-            there = slo.at[pl.ds(aligned(BASE[t] + p * CB[t], 16), CB[t])]
-            remote(there, there, slo_s.at[t, p], slo_r.at[t, p], {"mp": p}).wait_recv()
-            return _
-
-        lax.fori_loop(1, MP, slopes_in, 0)
+    first_relay(1)
+    second_relay(0)
+    first_relay(2)
+    second_relay(1)
+    second_relay(2)
+
+    for t in range(3):
+        got(t, place(pair, ring + turn[t]))
+        got(t, place(1 - pair, ring + 4 - turn[t]))
+        got(t, place(1 - pair, ring + turn[t]))
+        got(t, place(1 - pair, ring + 2))
         units = slice(t * HB, (t + 1) * HB)
         back = nn(heads[t][...], slo[BASE[t] : BASE[t] + WIDTHS[t], :])
         inner[units, :] = (back * before[units, :]).astype(BF16)
@@ -361,14 +420,19 @@
 
         lax.fori_loop(1, 8, body, 0)
 
+    def pieces(dst, j, value):
+        for k in range(4):
+            dst[j * 4 + k] = value[k * DB : (k + 1) * DB].astype(BF16)
+
     for t in range(3):
         def head_grad(i, _, t=t):
-            at = aligned(i * 128, 128)
-            rows = pl.ds(aligned(BASE[t] + at, 128), 128)
-            hf32[pl.ds(at, 128), :] = nt(slo[rows, :], lift[t * HB : (t + 1) * HB, :])
-            return _
-
-        lax.fori_loop(0, WIDTHS[t] // 128, head_grad, 0)
+            n = (384, 384, 640)[t]
+            at = aligned(i * n, 128)
+            rows = pl.ds(aligned(BASE[t] + at, 128), n)
+            hf32[pl.ds(at, n), :] = nt(slo[rows, :], lift[t * HB : (t + 1) * HB, :])
+            return _
+
+        lax.fori_loop(0, WIDTHS[t] // (384, 384, 640)[t], head_grad, 0)
 
         def head_piece(j, _, t=t):
             rows = pl.ds(aligned(j * PB[t], 8), PB[t])
@@ -379,10 +443,10 @@
     to_partner(0, hsend, hcore)
 
     def adaptor_grad(j, _):
-        asend[j] = nt(finalt[pl.ds(aligned(j * DB, 16), DB), :], inner[...]).astype(BF16)
-        return _
-
-    lax.fori_loop(0, DP, adaptor_grad, 0)
+        pieces(asend, j, nt(finalt[pl.ds(aligned(j * 4 * DB, 16), 4 * DB), :], inner[...]))
+        return _
+
+    lax.fori_loop(0, DP // 4, adaptor_grad, 0)
     to_partner(1, asend, acore)
     onward(0, hsend, hcore, hmid, hrecv)
     onward(1, asend, acore, amid, arecv)
@@ -399,24 +463,14 @@
     spread(thr, 3)
     arrived(thr, 3)
 
-    def flip_all(src):
-        def body(i, _):
-            at = aligned(i * 128, 128)
-            finalt[pl.ds(at, 128), :] = flipped(src[:, pl.ds(at, 128)])
-            return _
-
-        lax.fori_loop(0, D // 128, body, 0)
-
-    flip_all(thr)
+    flip_all(thr, finalt)
 
     def narrow_grad(j, _):
-        nsend[j] = nn(finalt[pl.ds(aligned(j * DB, 16), DB), :], active[...]).astype(BF16)
-        return _
-
-    lax.fori_loop(0, DP, narrow_grad, 0)
+        pieces(nsend, j, nn(finalt[pl.ds(aligned(j * 4 * DB, 16), 4 * DB), :], active[...]))
+        return _
+
+    lax.fori_loop(0, DP // 4, narrow_grad, 0)
     to_partner(2, nsend, ncore)
-    flip_all(first)
-
     def backward(i, _):
         rows = pl.ds(aligned(i * 128, 128), 128)
         active[rows, :] = (nt(thr[rows, :], nw[...]) * wide[rows, :]).astype(BF16)
@@ -426,14 +480,19 @@
     onward(2, nsend, ncore, nmid, nrecv)
 
     def widen_grad(j, _):
-        wsend[j] = nn(finalt[pl.ds(aligned(j * DB, 16), DB), :], active[...]).astype(BF16)
-        return _
-
-    lax.fori_loop(0, DP, widen_grad, 0)
+        pieces(wsend, j, nn(firstt[pl.ds(aligned(j * 4 * DB, 16), 4 * DB), :], active[...]))
+        return _
+
+    lax.fori_loop(0, DP // 4, widen_grad, 0)
     to_partner(3, wsend, wcore)
     onward(3, wsend, wcore, wmid, wrecv)
-    reduced(0, hmid, hrecv, out_h)
-    reduced(1, amid, arecv, out_a)
+    reduced(0, hmid, hrecv, hacc)
+    out_d[...] = hacc[0:96, :].T
+    out_g[...] = hacc[96:168, :]
+    out_s[...] = hacc[176:256, :].T
+    reduced(1, amid, arecv, aacc)
+    for t in range(3):
+        out_a[t] = aacc[:, t * HB : (t + 1) * HB]
     reduced(2, nmid, nrecv, out_n)
     reduced(3, wmid, wrecv, out_w)
 
@@ -454,10 +513,12 @@
             there = rs2.at[m, OFF[t] : OFF[t] + CB[t]]
             remote(sp.at[rows], there, stu_s.at[t, p], stu_r.at[t, m], where).wait_send()
             remote(stats.at[t], statr.at[t, m], sta_s.at[t, p], sta_r.at[t, m], where).wait_send()
-            remote(slo.at[rows], slo.at[rows], slo_s.at[t, p], slo_r.at[t, m], where).wait_send()
         return _
 
     lax.fori_loop(1, MP, sent_mp, 0)
+    for t in range(3):
+        for k in range(7):
+            slope_copy(t, m, k, place(pair, ring + 1)).wait_send()
     reductions = (
         (hsend, hcore, hmid, hrecv),
         (asend, acore, amid, arecv),
@@ -497,17 +558,26 @@
         ]
 
     dma = pltpu.SemaphoreType.DMA
-    w, n, a, h = pl.pallas_call(
+    arrays = (
+        tokens, widen_weight, narrow_weight,
+        teacher_dino.transpose(0, 2, 1), teacher_siglip.transpose(0, 2, 1), teacher_sam.transpose(0, 2, 1),
+        adaptor_in.transpose(0, 2, 1), head_dino, head_siglip, head_sam,
+    )
+    w, n, a, dino, siglip, sam = pl.pallas_call(
         kernel,
         out_shape=(
             jax.ShapeDtypeStruct((DB, FB), F32),
             jax.ShapeDtypeStruct((DB, FB), F32),
-            jax.ShapeDtypeStruct((DB, 3 * HB), F32),
-            jax.ShapeDtypeStruct((256, HB), F32),
+            jax.ShapeDtypeStruct((3, DB, HB), F32),
+            jax.ShapeDtypeStruct((HB, PB[0]), F32),
+            jax.ShapeDtypeStruct((PB[1], HB), F32),
+            jax.ShapeDtypeStruct((HB, PB[2]), F32),
         ),
-        in_specs=[pl.BlockSpec(memory_space=pltpu.SMEM)] + [vmem] * 13,
-        out_specs=(vmem,) * 4,
+        in_specs=[pl.BlockSpec(memory_space=pltpu.SMEM)] + [vmem] * 3 + [pl.BlockSpec(memory_space=pl.ANY)] * 10,
+        out_specs=(vmem,) * 6,
         scratch_shapes=[
+            *[pltpu.VMEM(array.shape, array.dtype) for array in arrays],
+            dma((len(arrays),)),
             pltpu.VMEM((R, D), BF16),
             pltpu.VMEM((R, FB), F32),
             pltpu.VMEM((R, FB), BF16),
@@ -533,7 +603,10 @@
             pltpu.VMEM((MP, BLK, D), BF16),
             pltpu.VMEM((R, D), BF16),
             pltpu.VMEM((D, R), BF16),
+            pltpu.VMEM((D, R), BF16),
             pltpu.VMEM((1536, HB), F32),
+            pltpu.VMEM((256, HB), F32),
+            pltpu.VMEM((DB, 3 * HB), F32),
             *reduction(256, HB),
             *reduction(DB, 3 * HB),
             *reduction(DB, FB),
@@ -551,18 +624,9 @@
         ),
         name="step",
     )(
-        step_lags, owner_slot[None], tokens, norm_gain[None], widen_weight, narrow_weight, final_gain[None],
-        adaptor_in.transpose(0, 2, 1), head_dino, head_siglip, head_sam,
-        teacher_dino.transpose(0, 2, 1), teacher_siglip.transpose(0, 2, 1), teacher_sam.transpose(0, 2, 1),
-    )
-    return (
-        w.T,
-        n.T,
-        a.reshape(DB, 3, HB).transpose(1, 0, 2),
-        h[0:96].T,
-        h[96:168].T,
-        h[176:256].T,
-    )
+        step_lags, owner_slot[None], norm_gain[None], final_gain[None], *arrays
+    )
+    return w.T, n.T, a, dino, siglip.T, sam
 
 
 def solution(mesh):

time: 249 us -> 230 us (0.924); the launches traced: 249 us -> 227 us
  Pallas kernels: 238 us -> 216 us
    pallas_call x1, Pallas kernels: 238 us -> 216 us  [local(): pl.pallas_call(kernel, out_shape=(jax.ShapeDtypeStruct((DB, FB), F32), ja...]
    unnamed x9 -> x8, local copies, waits for them, and re-layouts: 3.69 us -> 8.62 us
    transpose x3 -> x0, local copies, waits for them, and re-layouts: 3.36 us -> none  [the longest x1 1.57 us: local(): h[96:168]]
where the time goes in v2:
time: 230 us; the launch traced here: 227 us
  Pallas kernels  216 us (94%)
  local copies, waits for them, and re-layouts  11.2 us (5%)
    pallas_call x1, Pallas kernels, local(): pl.pallas_call(kernel, out_shape=(jax.ShapeDtypeStruct((DB, FB), F32), ja...  216 us
    unnamed x8, local copies, waits for them, and re-layouts  8.62 us

profile of v2, /device:TPU:24, one launch (start us, length us, event | category | flops | bytes accessed | tf_op | source)
XLA Modules:
  0.0 227.4 jit_solution(8298542948817031210)
XLA Ops:
  0.6 1.3 broadcast_in_dim.10.ng
  1.9 1.3 broadcast_in_dim.11.fg
  3.2 215.5 %step.1 = (f32[80,640]{1,0:T(8,128)}, f32[80,640]{1,0:T(8,128)}, f32[3,80,160]{2,1,0:T(8,128)}, f32[160,96]{1,0:T(8,128)}, f32[72,160]{1,0:T(8,128)}, /*index=5*/f32[160,80]{1,0:T(8,128)}) custom-call(s32[3]{0:T(128)} %lags.1, s32[1,256]{1,0:T(1,128)} %bitcast.15, f32[1,1280]{1,0:T(1,128)} %broadcast_in_dim.10.ng, f32[1,1280]{1,0:T(1,128)} %broadcast_in_dim.11.fg, ...), custom_call_target="tpu_custom_call" | custom-call | tf_op jit(solution)/shard_map/step/pallas_call | solution.py:566
  218.7 0.0 copy-start
  218.7 1.7 copy.26
  220.4 1.6 copy.27
  222.0 1.7 copy.28
  223.7 1.5 copy.29
  225.2 1.5 copy.30
  226.7 0.0 copy-done
  226.7 0.6 copy.31
Async XLA Ops:
  218.7 8.0 %copy-start = (f32[160,80]{1,0:T(8,128)S(1)}, f32[160,80]{1,0:T(8,128)}, u32[]{:S(2)}) copy-start(f32[160,80]{1,0:T(8,128)} %get-tuple-element.29) | copy-start | bytes 153604

commit v3 on v2

--- a/solution.py
+++ b/solution.py
@@ -243,25 +243,58 @@
 
     arrived(final, 1)
 
+    pair, ring = m // 4, lax.rem(m, 4)
+
+    def place(a, b):
+        return a * 4 + lax.rem(b, 4)
+
+    def channels(t, p):
+        return pl.ds(aligned(BASE[t] + p * CB[t], 16), CB[t])
+
+    def stu_copy(t, p, slot, k, to):
+        there = rs2.at[slot, OFF[t] : OFF[t] + CB[t]]
+        return remote(sp.at[channels(t, p)], there, stu_s.at[t, k], stu_r.at[t, slot], {"mp": to})
+
+    def stu_got(t, slot):
+        stu_copy(t, m, slot, slot, place(1 - pair, ring)).wait_recv()
+        return rs2[slot, OFF[t] : OFF[t] + CB[t]].astype(F32)
+
     for t in range(3):
         units = slice(t * HB, (t + 1) * HB)
         b = nt(ai[t], final[...])
         before[units, :] = b
         lift[units, :] = smooth(b).astype(BF16)
 
-        def student(i, _, t=t, units=units):
-            p = mate(i)
-            rows = pl.ds(aligned(BASE[t] + p * CB[t], 16), CB[t])
+        def student(p, t=t, units=units):
+            rows = channels(t, p)
             sp[rows, :] = nn(headt[rows, :], lift[units, :]).astype(BF16)
 
-            @pl.when(p != m)
-            def _send():
-                there = rs2.at[m, OFF[t] : OFF[t] + CB[t]]
-                remote(sp.at[rows], there, stu_s.at[t, p], stu_r.at[t, m], {"mp": p}).start()
-
-            return _
-
-        lax.fori_loop(1, MP + 1, student, 0)
+        if t == 0:
+            def over_pair(i, _, student=student):
+                y = lax.rem(ring + i, 4)
+                student(place(1 - pair, y))
+                stu_copy(0, place(1 - pair, y), y, y, place(1 - pair, ring)).start()
+                return _
+
+            def kept(i, _, student=student):
+                student(place(pair, ring + i))
+                return _
+
+            lax.fori_loop(0, 4, over_pair, 0)
+            lax.fori_loop(0, 4, kept, 0)
+        else:
+            def over_ring(i, _, t=t, student=student):
+                y, c = lax.rem(ring + 1 + i // 2, 4), lax.rem(i, 2)
+                student(place(c, y))
+                stu_copy(t, place(c, y), ring * 2 + c, y * 2 + c, place(pair, y)).start()
+                return _
+
+            def kept(i, _, student=student):
+                student(place(i, ring))
+                return _
+
+            lax.fori_loop(0, 6, over_ring, 0)
+            lax.fori_loop(0, 2, kept, 0)
 
     slopes_of(before, 3 * HB)
 
@@ -276,18 +309,37 @@
     flip_all(final, finalt)
     flip_all(first, firstt)
 
+    def half_summed(t):
+        mine = slice(OFF[t], OFF[t] + CB[t])
+        if t == 0:
+            def body(i, _):
+                y = lax.rem(ring + i, 4)
+                rows = channels(0, place(pair, y))
+                sp[rows, :] = (sp[rows, :].astype(F32) + stu_got(0, y)).astype(BF16)
+                stu_copy(0, place(pair, y), 4 + ring, 4 + y, place(pair, y)).start()
+                return _
+
+            lax.fori_loop(1, 4, body, 0)
+            stu[mine, :] = sp[channels(0, m), :].astype(F32) + stu_got(0, ring)
+        else:
+            other = channels(t, place(1 - pair, ring))
+            total = sp[other, :].astype(F32)
+            for i in range(1, 4):
+                total = total + stu_got(t, lax.rem(ring + i, 4) * 2 + 1 - pair)
+            sp[other, :] = total.astype(BF16)
+            stu_copy(t, place(1 - pair, ring), ring * 2, ring * 2, place(1 - pair, ring)).start()
+            total = sp[channels(t, m), :].astype(F32)
+            for i in range(1, 4):
+                total = total + stu_got(t, lax.rem(ring + i, 4) * 2 + pair)
+            stu[mine, :] = total
+
     def gather_student(t):
         mine = slice(OFF[t], OFF[t] + CB[t])
-        stu[mine, :] = sp[pl.ds(aligned(BASE[t] + m * CB[t], 16), CB[t]), :].astype(F32)
-
-        def body(i, _):
-            p = mate(i)
-            here = rs2.at[p, mine]
-            remote(here, here, stu_s.at[t, p], stu_r.at[t, p], {"mp": p}).wait_recv()
-            stu[mine, :] += rs2[p, mine].astype(F32)
-            return _
-
-        lax.fori_loop(1, MP, body, 0)
+        if t == 0:
+            for i in range(1, 4):
+                stu[mine, :] += stu_got(0, 4 + lax.rem(ring + i, 4))
+        else:
+            stu[mine, :] += stu_got(t, ring * 2)
         y = stu[mine, :]
         f = tgt[mine, :].astype(F32)
         stats[t, 0:1, :] = jnp.sum(y * f, axis=0, keepdims=True)
@@ -319,11 +371,7 @@
         pass_on(t, m, 1, place(pair, ring + 3))
         pass_on(t, m, 2, place(1 - pair, ring))
 
-    pair, ring = m // 4, lax.rem(m, 4)
     turn = (1, 3, 3)
-
-    def place(a, b):
-        return a * 4 + lax.rem(b, 4)
 
     def slope_copy(t, owner, k, to):
         block = slo.at[pl.ds(aligned(BASE[t] + owner * CB[t], 16), CB[t])]
@@ -349,20 +397,23 @@
         got(t, owner)
         pass_on(t, owner, 6, place(1 - pair, ring))
 
+    half_summed(1)
+    half_summed(0)
+    gather_student(1)
+    half_summed(2)
+    slope(1)
     gather_student(0)
-    gather_student(1)
+    gather_student(2)
+    first_relay(1)
     slope(0)
-    gather_student(2)
-    slope(1)
+    slope(2)
     first_relay(0)
-    slope(2)
-    first_relay(1)
+    second_relay(1)
+    first_relay(2)
     second_relay(0)
-    first_relay(2)
-    second_relay(1)
     second_relay(2)
 
-    for t in range(3):
+    for t in (1, 0, 2):
         got(t, place(pair, ring + turn[t]))
         got(t, place(1 - pair, ring + 4 - turn[t]))
         got(t, place(1 - pair, ring + turn[t]))
@@ -509,9 +560,6 @@
         for which, (src, dst) in enumerate(((part, rs1), (final, rs1), (part2, rs3), (thr, rs3))):
             remote(src.at[own_rows], dst.at[m], row_s.at[which, p], row_r.at[which, m], where).wait_send()
         for t in range(3):
-            rows = pl.ds(aligned(BASE[t] + p * CB[t], 16), CB[t])
-            there = rs2.at[m, OFF[t] : OFF[t] + CB[t]]
-            remote(sp.at[rows], there, stu_s.at[t, p], stu_r.at[t, m], where).wait_send()
             remote(stats.at[t], statr.at[t, m], sta_s.at[t, p], sta_r.at[t, m], where).wait_send()
         return _
 
@@ -519,6 +567,16 @@
     for t in range(3):
         for k in range(7):
             slope_copy(t, m, k, place(pair, ring + 1)).wait_send()
+        for i in range(1, 4):
+            y = lax.rem(ring + i, 4)
+            if t == 0:
+                stu_copy(0, m, y, y, place(1 - pair, ring)).wait_send()
+                stu_copy(0, m, y, 4 + y, place(1 - pair, ring)).wait_send()
+            else:
+                stu_copy(t, m, y, y * 2, place(1 - pair, ring)).wait_send()
+                stu_copy(t, m, y, y * 2 + 1, place(1 - pair, ring)).wait_send()
+        k = ring if t == 0 else ring * 2
+        stu_copy(t, m, k, k, place(1 - pair, ring)).wait_send()
     reductions = (
         (hsend, hcore, hmid, hrecv),
         (asend, acore, amid, arecv),

time: 230 us -> 222 us (0.965)
  Pallas kernels: 216 us -> 208 us
    pallas_call x1, Pallas kernels: 216 us -> 208 us  [local(): pl.pallas_call(kernel, out_shape=(jax.ShapeDtypeStruct((DB, FB), F32), ja...]
where the time goes in v3:
time: 222 us; the launch traced here: 219 us
  Pallas kernels  208 us (94%)
  local copies, waits for them, and re-layouts  11.2 us (5%)
    pallas_call x1, Pallas kernels, local(): pl.pallas_call(kernel, out_shape=(jax.ShapeDtypeStruct((DB, FB), F32), ja...  208 us
    unnamed x8, local copies, waits for them, and re-layouts  8.62 us

profile of v3, /device:TPU:24, one launch (start us, length us, event | category | flops | bytes accessed | tf_op | source)
XLA Modules:
  0.0 219.5 jit_solution(4476699923383399835)
XLA Ops:
  0.6 1.3 broadcast_in_dim.10.ng
  1.9 1.3 broadcast_in_dim.11.fg
  3.2 207.6 %step.1 = (f32[80,640]{1,0:T(8,128)}, f32[80,640]{1,0:T(8,128)}, f32[3,80,160]{2,1,0:T(8,128)}, f32[160,96]{1,0:T(8,128)}, f32[72,160]{1,0:T(8,128)}, /*index=5*/f32[160,80]{1,0:T(8,128)}) custom-call(s32[3]{0:T(128)} %lags.1, s32[1,256]{1,0:T(1,128)} %bitcast.15, f32[1,1280]{1,0:T(1,128)} %broadcast_in_dim.10.ng, f32[1,1280]{1,0:T(1,128)} %broadcast_in_dim.11.fg, ...), custom_call_target="tpu_custom_call" | custom-call | tf_op jit(solution)/shard_map/step/pallas_call | solution.py:624
  210.9 0.0 copy-start
  210.9 1.7 copy.26
  212.5 1.6 copy.27
  214.2 1.7 copy.28
  215.8 1.5 copy.29
  217.3 1.5 copy.30
  218.9 0.0 copy-done
  218.9 0.6 copy.31
Async XLA Ops:
  210.9 8.0 %copy-start = (f32[160,80]{1,0:T(8,128)S(1)}, f32[160,80]{1,0:T(8,128)}, u32[]{:S(2)}) copy-start(f32[160,80]{1,0:T(8,128)} %get-tuple-element.29) | copy-start | bytes 153604

commit v4 on v3

--- a/solution.py
+++ b/solution.py
@@ -475,6 +475,47 @@
         for k in range(4):
             dst[j * 4 + k] = value[k * DB : (k + 1) * DB].astype(BF16)
 
+    side, level = half // 4, lax.rem(half, 4)
+
+    def chip(a, b):
+        return {"dp": (a * 4 + b) * 2 + core}
+
+    def along(which, mid, last, k, slot, send, to):
+        return remote(mid.at[k], last.at[slot], dp_s.at[which, send], dp_r.at[which, slot], to)
+
+    def along_z(which, send, received, mid, last):
+        def body(i, _):
+            z, a = lax.rem(level + 1 + i // 2, 4), lax.rem(i, 2)
+            k = a * 4 + z
+            remote(send.at[k], received.at[k], cor_s.at[which, k], cor_r.at[which, k], {"dp": partner}).wait_recv()
+            mid[k] = (send[k * 2 + core].astype(F32) + received[k].astype(F32)).astype(BF16)
+
+            @pl.when(z != level)
+            def _send():
+                along(which, mid, last, k, level * 2 + a, z * 2 + a, chip(side, z)).start()
+
+            return _
+
+        lax.fori_loop(0, 8, body, 0)
+
+    def z_sum(which, mid, last, a):
+        total = mid[a * 4 + level].astype(F32)
+        for i in range(1, 4):
+            z = lax.rem(level + i, 4)
+            along(which, mid, last, 0, z * 2 + a, 0, chip(side, z)).wait_recv()
+            total = total + last[z * 2 + a].astype(F32)
+        return total
+
+    def over_x(which, mid, last):
+        k = (1 - side) * 4 + level
+        mid[k] = z_sum(which, mid, last, 1 - side).astype(BF16)
+        along(which, mid, last, k, level * 2, level * 2, chip(1 - side, level)).start()
+
+    def reduced_zx(which, mid, last, out):
+        total = z_sum(which, mid, last, side)
+        along(which, mid, last, 0, level * 2, 0, chip(1 - side, level)).wait_recv()
+        out[...] = total + last[level * 2].astype(F32)
+
     for t in range(3):
         def head_grad(i, _, t=t):
             n = (384, 384, 640)[t]
@@ -499,8 +540,8 @@
 
     lax.fori_loop(0, DP // 4, adaptor_grad, 0)
     to_partner(1, asend, acore)
-    onward(0, hsend, hcore, hmid, hrecv)
-    onward(1, asend, acore, amid, arecv)
+    along_z(0, hsend, hcore, hmid, hrecv)
+    along_z(1, asend, acore, amid, arecv)
 
     upstream = gathered(part2, 2, rs3)
     scaled = upstream * fg[...]
@@ -512,6 +553,8 @@
     )
     thr[own_rows, :] = through.astype(BF16)
     spread(thr, 3)
+    over_x(0, hmid, hrecv)
+    over_x(1, amid, arecv)
     arrived(thr, 3)
 
     flip_all(thr, finalt)
@@ -537,11 +580,11 @@
     lax.fori_loop(0, DP // 4, widen_grad, 0)
     to_partner(3, wsend, wcore)
     onward(3, wsend, wcore, wmid, wrecv)
-    reduced(0, hmid, hrecv, hacc)
+    reduced_zx(0, hmid, hrecv, hacc)
     out_d[...] = hacc[0:96, :].T
     out_g[...] = hacc[96:168, :]
     out_s[...] = hacc[176:256, :].T
-    reduced(1, amid, arecv, aacc)
+    reduced_zx(1, amid, arecv, aacc)
     for t in range(3):
         out_a[t] = aacc[:, t * HB : (t + 1) * HB]
     reduced(2, nmid, nrecv, out_n)
@@ -593,11 +636,17 @@
 
     def sent_chip(i, _):
         k = lax.rem(half + i, 8)
-        for which, (send, received, mid, last) in enumerate(reductions):
+        for which, (send, received, mid, last) in list(enumerate(reductions))[2:]:
             remote(mid.at[k], last.at[half], dp_s.at[which, k], dp_r.at[which, half], {"dp": k * 2 + core}).wait_send()
         return _
 
     lax.fori_loop(1, 8, sent_chip, 0)
+    for which, (send, received, mid, last) in list(enumerate(reductions))[:2]:
+        for i in range(1, 4):
+            z = lax.rem(level + i, 4)
+            for a in range(2):
+                along(which, mid, last, 0, 0, z * 2 + a, chip(1 - side, level)).wait_send()
+        along(which, mid, last, 0, 0, level * 2, chip(1 - side, level)).wait_send()
 
 
 def local(

time: 222 us -> 205 us (0.923)
  Pallas kernels: 208 us -> 191 us
    pallas_call x1, Pallas kernels: 208 us -> 191 us  [local(): pl.pallas_call(kernel, out_shape=(jax.ShapeDtypeStruct((DB, FB), F32), ja...]
where the time goes in v4:
time: 205 us; the launch traced here: 203 us
  Pallas kernels  191 us (93%)
  local copies, waits for them, and re-layouts  11.2 us (5%)
    pallas_call x1, Pallas kernels, local(): pl.pallas_call(kernel, out_shape=(jax.ShapeDtypeStruct((DB, FB), F32), ja...  191 us
    unnamed x8, local copies, waits for them, and re-layouts  8.62 us

profile of v4, /device:TPU:24, one launch (start us, length us, event | category | flops | bytes accessed | tf_op | source)
XLA Modules:
  0.0 202.9 jit_solution(1842017820860140768)
XLA Ops:
  0.6 1.3 broadcast_in_dim.10.ng
  1.9 1.3 broadcast_in_dim.11.fg
  3.2 191.0 %step.1 = (f32[80,640]{1,0:T(8,128)}, f32[80,640]{1,0:T(8,128)}, f32[3,80,160]{2,1,0:T(8,128)}, f32[160,96]{1,0:T(8,128)}, f32[72,160]{1,0:T(8,128)}, /*index=5*/f32[160,80]{1,0:T(8,128)}) custom-call(s32[3]{0:T(128)} %lags.1, s32[1,256]{1,0:T(1,128)} %bitcast.15, f32[1,1280]{1,0:T(1,128)} %broadcast_in_dim.10.ng, f32[1,1280]{1,0:T(1,128)} %broadcast_in_dim.11.fg, ...), custom_call_target="tpu_custom_call" | custom-call | tf_op jit(solution)/shard_map/step/pallas_call | solution.py:673
  194.3 0.0 copy-start
  194.3 1.7 copy.26
  195.9 1.6 copy.27
  197.5 1.7 copy.28
  199.2 1.5 copy.29
  200.7 1.5 copy.30
  202.2 0.0 copy-done
  202.2 0.6 copy.31
Async XLA Ops:
  194.3 8.0 %copy-start = (f32[160,80]{1,0:T(8,128)S(1)}, f32[160,80]{1,0:T(8,128)}, u32[]{:S(2)}) copy-start(f32[160,80]{1,0:T(8,128)} %get-tuple-element.29) | copy-start | bytes 153604
